TPU v7x, 32 devices: a whole 2x2x4 slice. The times are simulated.
32 devices in a mesh: dp: 8 (over z, x), tensor: 4 (over y, core).
Axes of the slice: x: 2, y: 2, z: 4, core: 2. Of those that a mesh axis runs over, the one named last changes fastest.
Arguments:
- tokens: bfloat16 [512, 4096], P('dp', 'tensor')
- norm_gain: float32 [4096], P('tensor'), may hold values from 0.5 to 1.5
- eraser_mean: float32 [4096], P('tensor'), may hold values from -6 to 6
- eraser_in: float32 [4096, 128], P('tensor'), may hold values from -0.09375 to 0.09375
- eraser_out: float32 [4096, 128], P('tensor'), may hold values from -0.5 to 0.5
- router: float32 [4096, 8], P('tensor'), may hold values from -0.09375 to 0.09375
- expert_ids: int32 [512, 2], P('dp'), may hold values from 0 to 7, as said below
- slots: int32 [512, 2], P('dp'), may hold values from 0 to 63, as said below
- w_gate: bfloat16 [8, 4096, 14336], P('dp', None, 'tensor'), may hold values from -0.09375 to 0.09375
- w_up: bfloat16 [8, 4096, 14336], P('dp', None, 'tensor'), may hold values from -0.09375 to 0.09375
- w_down: bfloat16 [8, 14336, 4096], P('dp', 'tensor'), may hold values from -0.0625 to 0.0625
Outputs:
- moe_out: bfloat16 [512, 4096], P('dp', 'tensor')
Inputs may be any that keep to these rules, and one draw needn't show every extreme that they name: `expert_ids`: the two experts of a token differ. Within each aligned block of 64 tokens, the choices naming one expert have the slots 0, 1, 2, ... with no repeats; choices with a slot of 24 or more are dropped.
All inputs are finite; a program needn't handle non-finite values.
Results may differ from a plain program's by a relative error of at most 0.0065.
Values may be sent and summed in bfloat16 or wider, within the bound.
A program may use at most 128 MiB of HBM per device.

v0:
```python
import jax
import jax.numpy as jnp
from jax import lax
from jax.sharding import PartitionSpec as P

E = 8


def on_device(
    tokens,
    norm_gain,
    eraser_mean,
    eraser_in,
    eraser_out,
    router,
    expert_ids,
    slots,
    w_gate,
    w_up,
    w_down,
):
    highest = lax.Precision.HIGHEST
    part_count = lax.axis_size("dp") // E
    tok_rows = tokens.shape[0]
    capacity = 3 * tok_rows // 8
    width = tokens.shape[1] * lax.axis_size("tensor")
    values = tokens.astype(jnp.float32)
    gained = values * norm_gain[None, :]
    squares = jnp.sum(values * values, axis=1)
    gained_in = jnp.dot(gained, eraser_in, precision=highest, preferred_element_type=jnp.float32)
    mean_in = jnp.dot(
        eraser_mean[None, :], eraser_in, precision=highest, preferred_element_type=jnp.float32
    )[0]
    squares, gained_in, mean_in = lax.psum((squares, gained_in, mean_in), "tensor")
    inv_rms = lax.rsqrt(squares / width + 1e-05)
    projected = inv_rms[:, None] * gained_in - mean_in[None, :]
    cleaned = inv_rms[:, None] * gained - jnp.dot(
        projected, eraser_out.T, precision=highest, preferred_element_type=jnp.float32
    )
    logits = lax.psum(
        jnp.dot(cleaned, router, precision=highest, preferred_element_type=jnp.float32), "tensor"
    )
    erased = cleaned.astype(jnp.bfloat16)
    chosen = (expert_ids[:, :, None] == jnp.arange(E, dtype=jnp.int32)[None, None, :]).astype(
        jnp.float32
    )
    picked = jnp.sum(chosen * logits[:, None, :], axis=2)
    first_gate = jax.nn.sigmoid(picked[:, 0] - picked[:, 1])
    gate_pair = jnp.stack([first_gate, 1.0 - first_gate], axis=1)
    kept_mask = slots < capacity
    target = expert_ids * capacity + slots
    columns = jnp.arange(E * capacity, dtype=jnp.int32)
    match = ((target[:, :, None] == columns[None, None, :]) & kept_mask[:, :, None]).astype(
        jnp.float32
    )
    placing = jnp.sum(match, axis=1).T.astype(jnp.bfloat16)
    weights = jnp.sum(match * gate_pair[:, :, None], axis=1)
    full_rows = lax.all_gather(erased, "tensor", axis=1, tiled=True)
    filled = jnp.dot(placing, full_rows, preferred_element_type=jnp.float32).astype(jnp.bfloat16)
    received = lax.all_to_all(
        jnp.repeat(filled.reshape(E, capacity, full_rows.shape[1]), part_count, axis=0),
        "dp",
        split_axis=0,
        concat_axis=0,
        tiled=True,
    )
    sources, count, features = received.shape
    flat_rows = received.reshape(sources * count, features)
    gate_act = jnp.dot(flat_rows, w_gate[0], preferred_element_type=jnp.float32)
    up_act = jnp.dot(flat_rows, w_up[0], preferred_element_type=jnp.float32)
    hidden = (jax.nn.silu(gate_act) * up_act).astype(jnp.bfloat16)
    outputs = jnp.dot(hidden, w_down[0], preferred_element_type=jnp.float32).reshape(
        sources, count, features
    )
    reduced = lax.psum_scatter(outputs, "tensor", scatter_dimension=2, tiled=True)
    returned = lax.all_to_all(reduced, "dp", split_axis=0, concat_axis=0, tiled=True)
    summed = jnp.sum(returned.reshape(E, part_count, capacity, returned.shape[2]), axis=1).reshape(
        E * capacity, returned.shape[2]
    )
    mixed = jnp.dot(weights, summed, precision=highest, preferred_element_type=jnp.float32)
    return mixed.astype(jnp.bfloat16)


def solution(mesh):
    in_specs = (
        P("dp", "tensor"),
        P("tensor"),
        P("tensor"),
        P("tensor", None),
        P("tensor", None),
        P("tensor", None),
        P("dp", None),
        P("dp", None),
        P("dp", None, "tensor"),
        P("dp", None, "tensor"),
        P("dp", "tensor", None),
    )
    out_specs = P("dp", "tensor")
    return jax.shard_map(
        on_device, mesh=mesh, in_specs=in_specs, out_specs=out_specs, check_vma=False
    )
```

profile of v0, /device:TPU:0, one launch (start us, length us, event | category | flops | bytes accessed | tf_op | source)
XLA Modules:
  0.0 193.4 jit_solution(11568342095001069763)
XLA Ops:
  6.5 0.0 copy-start
  6.5 0.0 copy-start.2
  6.5 0.0 reduce-scatter.2.cloned.1.call-start
  6.5 0.7 broadcast_compare_fusion
  7.3 1.0 fusion.14
  8.3 0.7 multiply_add_fusion
  9.0 1.4 convolution_bitcast_fusion
  10.4 1.6 fusion.12
  12.0 13.2 %all-reduce = (f32[64]{0:T(128)S(1)}, f32[64,128]{1,0:T(8,128)S(1)}, f32[128]{0:T(128)S(1)}) all-reduce(f32[64]{0:T(128)S(1)} %fusion.14, f32[64,128]{1,0:T(8,128)S(1)} %fusion.12, f32[128]{0:T(128)S(1)} %convolution_bitcast_fusion), channel_id=1, replica_groups=mesh['dp'=8,'tensor'=4] {'tensor'}, use_global_device_ids=true, to_apply=%region_1.0 | all-reduce | flops 8384 | bytes 67072 | tf_op jit(solution)/shard_map/psum | solution.py:34
  25.2 0.0 copy-done
  25.2 1.6 fusion.22
  26.9 1.0 fusion.23
  27.9 5.8 %psum.31 = f32[64,8]{0,1:T(8,128)S(1)} all-reduce(f32[64,8]{0,1:T(8,128)S(1)} %fusion.23), channel_id=1, replica_groups=mesh['dp'=8,'tensor'=4] {'tensor'}, use_global_device_ids=true, to_apply=%region_4.0 | all-reduce | flops 512 | bytes 4096 | tf_op jit(solution)/shard_map/psum | solution.py:40
  33.7 0.0 copy-done.2
  33.7 6.7 %all_gather.3 = bf16[64,4096]{1,0:T(8,128)(2,1)S(1)} all-gather(bf16[64,1024]{1,0:T(8,128)(2,1)S(1)} %get-tuple-element.12), channel_id=1, replica_groups=mesh['dp'=8,'tensor'=4] {'tensor'}, dimensions={1}, use_global_device_ids=true | all-gather | bytes 655360 | tf_op jit(solution)/shard_map/all_gather | solution.py:58
  40.4 0.1 convert_reduce_fusion
  40.6 0.6 convolution_convert_fusion
  41.2 43.1 %all_to_all.10 = bf16[8,24,4096]{2,1,0:T(8,128)(2,1)S(1)} all-to-all(bf16[8,24,4096]{2,1,0:T(8,128)(2,1)S(1)} %bitcast.34), channel_id=1, replica_groups=mesh['dp'=8,'tensor'=4] {'dp'}, dimensions={0} | all-to-all | bytes 3145728 | tf_op jit(solution)/shard_map/all_to_all | solution.py:60
  84.2 12.4 %fusion.4 = f32[192,3584]{1,0:T(8,128)S(1)} fusion(bf16[192,4096]{1,0:T(8,128)(2,1)S(1)} %bitcast.36, bf16[1,4096,3584]{2,1,0:T(8,128)(2,1)} %param.19), kind=kOutput, calls=%fused_computation.4 | convolution fusion | flops 5637144576 | bytes 33685504 | tf_op jit(solution)/shard_map/dot_general | solution.py:69
  96.7 12.5 %fusion.9 = bf16[192,3584]{1,0:T(8,128)(2,1)S(1)} fusion(bf16[192,4096]{1,0:T(8,128)(2,1)S(1)} %bitcast.37, bf16[1,4096,3584]{2,1,0:T(8,128)(2,1)} %param.20, f32[192,3584]{1,0:T(8,128)S(1)} %fusion.4), kind=kOutput, calls=%fused_computation.7 | convolution fusion | flops 5641273344 | bytes 35061760 | tf_op jit(solution)/shard_map/dot_general | solution.py:70
  109.2 14.1 %fusion = f32[8,24,4096]{2,1,0:T(8,128)} fusion(bf16[8,24,3584]{2,1,0:T(8,128)(2,1)S(1)} %bitcast.39, bf16[1,3584,4096]{2,1,0:T(8,128)(2,1)} %param.21), kind=kOutput, calls=%fused_computation | convolution fusion | flops 5637144576 | bytes 33882112 | tf_op jit(solution)/shard_map/dot_general | solution.py:72
  123.3 0.0 copy-start.1
  123.3 0.0 reduce-scatter.2.cloned.1.call-update
  123.3 36.5 %reduce-scatter.2.cloned.1.call-done = f32[8,24,1024]{2,1,0:T(8,128)} async-done(((f32[8,24,4096]{2,1,0:T(8,128)}), f32[8,24,1024]{2,1,0:T(8,128)}) %reduce-scatter.2.cloned.1.call-update) | async-done | bytes 786448 | tf_op jit(solution)/shard_map/reduce_scatter | solution.py:75
  159.8 25.5 %all_to_all.11 = f32[8,24,1024]{2,1,0:T(8,128)S(1)} all-to-all(f32[8,24,1024]{2,1,0:T(8,128)} %reduce-scatter.2.cloned.1.call-done), channel_id=1, replica_groups=mesh['dp'=8,'tensor'=4] {'dp'}, dimensions={0} | all-to-all | bytes 1572864 | tf_op jit(solution)/shard_map/all_to_all | solution.py:76
  185.2 1.3 convolution_convert_fusion.1
  186.5 0.0 copy-done.1
  (4 shorter events, 0.0 us)
Async XLA Ops:
  6.5 18.7 %copy-start = (f32[1024,128]{1,0:T(8,128)S(1)}, f32[1024,128]{1,0:T(8,128)}, u32[]{:S(2)}) copy-start(f32[1024,128]{1,0:T(8,128)} %param.15) | copy-start | bytes 1572868
  6.5 27.2 %copy-start.2 = (s32[64,2]{0,1:T(2,128)S(1)}, s32[64,2]{0,1:T(2,128)}, u32[]{:S(2)}) copy-start(s32[64,2]{0,1:T(2,128)} %param.17) | copy-start | bytes 1540
  6.5 153.2 %reduce-scatter.2.cloned.1.call-start = ((), (), s32[]{:S(2)}) async-start(), calls=%async_computation.3 | async-start | bytes 3932160 | tf_op jit(solution)/shard_map/reduce_scatter | solution.py:75
  123.3 63.2 %copy-start.1 = (f32[1024,128]{1,0:T(8,128)S(1)}, f32[1024,128]{1,0:T(8,128)}, u32[]{:S(2)}) copy-start(f32[1024,128]{1,0:T(8,128)} %param.15) | copy-start | bytes 1572868
Sparse Core Ops, SparseCore 0:
  123.4 36.3 reduce-scatter.1
where the time goes:
time: 194 us; the launch traced here: 193 us
  blocking collectives  94.2 us (49%)
  matrix products  46.5 us (24%)
  waiting for transfers between devices  36.5 us (19%)
  between operations  13.5 us (7%)
  other arithmetic  2.64 us (1%)
    all_to_all x1, blocking collectives, on_device(): lax.all_to_all(jnp.repeat(filled.reshape(E, capacity, full_rows.shape[1])...  43.1 us
    reduce_scatter x1, waiting for transfers between devices, on_device(): lax.psum_scatter(outputs, 'tensor', scatter_dimension=2, tiled=True)  36.5 us
    all_to_all x1, blocking collectives, on_device(): lax.all_to_all(reduced, 'dp', split_axis=0, concat_axis=0, tiled=True)  25.5 us
    dot_general x1, matrix products, on_device(): jnp.dot(hidden, w_down[0], preferred_element_type=jnp.float32)  14.1 us
    psum x1, blocking collectives, on_device(): lax.psum((squares, gained_in, mean_in), 'tensor')  13.2 us
    dot_general x1, matrix products, on_device(): up_act = jnp.dot(flat_rows, w_up[0], preferred_element_type=jnp.float32)  12.5 us
    dot_general x1, matrix products, on_device(): gate_act = jnp.dot(flat_rows, w_gate[0], preferred_element_type=jnp.float32)  12.4 us
    all_gather x1, blocking collectives, on_device(): full_rows = lax.all_gather(erased, 'tensor', axis=1, tiled=True)  6.7 us
  transfers between devices with their start and end apart: 1, of which 1 were waited for; matrix products, arithmetic and copies ran while one was open for 0% of the time, Pallas kernels for 0%

commit v1 on v0

--- a/solution.py
+++ b/solution.py
@@ -30,15 +30,31 @@
     gained_in = jnp.dot(gained, eraser_in, precision=highest, preferred_element_type=jnp.float32)
     mean_in = jnp.dot(
         eraser_mean[None, :], eraser_in, precision=highest, preferred_element_type=jnp.float32
-    )[0]
-    squares, gained_in, mean_in = lax.psum((squares, gained_in, mean_in), "tensor")
+    )
+    router_out = jnp.dot(
+        router.T, eraser_out, precision=highest, preferred_element_type=jnp.float32
+    )
+    routed = jnp.dot(
+        router.T, gained.T, precision=highest, preferred_element_type=jnp.float32
+    )
+    rank = eraser_in.shape[1]
+    narrow = jnp.concatenate([routed, squares[None, :]], axis=0)
+    narrow = jnp.pad(narrow, ((0, 0), (0, rank - tok_rows)))
+    packed = lax.psum(
+        jnp.concatenate([gained_in, router_out, mean_in, narrow], axis=0), "tensor"
+    )
+    gained_in = packed[:tok_rows]
+    router_out = packed[tok_rows : tok_rows + E]
+    mean_in = packed[tok_rows + E]
+    routed = packed[tok_rows + E + 1 : tok_rows + 2 * E + 1, :tok_rows].T
+    squares = packed[tok_rows + 2 * E + 1, :tok_rows]
     inv_rms = lax.rsqrt(squares / width + 1e-05)
     projected = inv_rms[:, None] * gained_in - mean_in[None, :]
     cleaned = inv_rms[:, None] * gained - jnp.dot(
         projected, eraser_out.T, precision=highest, preferred_element_type=jnp.float32
     )
-    logits = lax.psum(
-        jnp.dot(cleaned, router, precision=highest, preferred_element_type=jnp.float32), "tensor"
+    logits = inv_rms[:, None] * routed - jnp.dot(
+        projected, router_out.T, precision=highest, preferred_element_type=jnp.float32
     )
     erased = cleaned.astype(jnp.bfloat16)
     chosen = (expert_ids[:, :, None] == jnp.arange(E, dtype=jnp.int32)[None, None, :]).astype(
@@ -55,15 +71,15 @@
     )
     placing = jnp.sum(match, axis=1).T.astype(jnp.bfloat16)
     weights = jnp.sum(match * gate_pair[:, :, None], axis=1)
-    full_rows = lax.all_gather(erased, "tensor", axis=1, tiled=True)
-    filled = jnp.dot(placing, full_rows, preferred_element_type=jnp.float32).astype(jnp.bfloat16)
+    filled = jnp.dot(placing, erased, preferred_element_type=jnp.float32).astype(jnp.bfloat16)
     received = lax.all_to_all(
-        jnp.repeat(filled.reshape(E, capacity, full_rows.shape[1]), part_count, axis=0),
+        jnp.repeat(filled.reshape(E, capacity, erased.shape[1]), part_count, axis=0),
         "dp",
         split_axis=0,
         concat_axis=0,
         tiled=True,
     )
+    received = lax.all_gather(received, "tensor", axis=2, tiled=True)
     sources, count, features = received.shape
     flat_rows = received.reshape(sources * count, features)
     gate_act = jnp.dot(flat_rows, w_gate[0], preferred_element_type=jnp.float32)
@@ -71,10 +87,10 @@
     hidden = (jax.nn.silu(gate_act) * up_act).astype(jnp.bfloat16)
     outputs = jnp.dot(hidden, w_down[0], preferred_element_type=jnp.float32).reshape(
         sources, count, features
-    )
+    ).astype(jnp.bfloat16)
     reduced = lax.psum_scatter(outputs, "tensor", scatter_dimension=2, tiled=True)
     returned = lax.all_to_all(reduced, "dp", split_axis=0, concat_axis=0, tiled=True)
-    summed = jnp.sum(returned.reshape(E, part_count, capacity, returned.shape[2]), axis=1).reshape(
+    summed = jnp.sum(returned.astype(jnp.float32).reshape(E, part_count, capacity, returned.shape[2]), axis=1).reshape(
         E * capacity, returned.shape[2]
     )
     mixed = jnp.dot(weights, summed, precision=highest, preferred_element_type=jnp.float32)

time: 194 us -> 160 us (0.82)
  blocking collectives: 94.2 us -> 47.4 us
  waiting for transfers between devices: 36.5 us -> 46.9 us
  matrix products: 46.5 us -> 50.6 us
    all_to_all x1, blocking collectives: 43.1 us -> 16.7 us  [on_device(): lax.all_to_all(jnp.repeat(filled.reshape(E, capacity, erased.shape[1]), p...]
    all_gather x0 -> x1, waiting for transfers between devices: none -> 18.7 us  [on_device(): received = lax.all_gather(received, 'tensor', axis=2, tiled=True)]
    reduce_scatter x1, waiting for transfers between devices: 36.5 us -> 28.1 us  [on_device(): lax.psum_scatter(outputs, 'tensor', scatter_dimension=2, tiled=True)]
    all_to_all x1, blocking collectives: 25.5 us -> 17.4 us  [on_device(): lax.all_to_all(reduced, 'dp', split_axis=0, concat_axis=0, tiled=True)]
    all_gather x1 -> x0, blocking collectives: 6.7 us -> none  [on_device(): full_rows = lax.all_gather(erased, 'tensor', axis=1, tiled=True)]
    psum x2 -> x1, blocking collectives: 19 us -> 13.2 us  [on_device(): lax.psum(jnp.concatenate([gained_in, router_out, mean_in, narrow], axis=0...]
    dot_general x1, matrix products: 12.4 us -> 15.9 us  [on_device(): gate_act = jnp.dot(flat_rows, w_gate[0], preferred_element_type=jnp.float32)]
  transfers between devices with their start and end apart: 1 -> 2, of which waited for: 1 -> 2; matrix products, arithmetic and copies ran while one was open for 0% -> 0% of each run, Pallas kernels for 0% -> 0%
where the time goes in v1:
time: 160 us
  matrix products  50.6 us (32%)
  blocking collectives  47.4 us (30%)
  waiting for transfers between devices  46.9 us (29%)
  between operations  13.5 us (8%)
    reduce_scatter x1, waiting for transfers between devices, on_device(): lax.psum_scatter(outputs, 'tensor', scatter_dimension=2, tiled=True)  28.1 us
    all_gather x1, waiting for transfers between devices, on_device(): received = lax.all_gather(received, 'tensor', axis=2, tiled=True)  18.7 us
    all_to_all x1, blocking collectives, on_device(): lax.all_to_all(reduced, 'dp', split_axis=0, concat_axis=0, tiled=True)  17.4 us
    all_to_all x1, blocking collectives, on_device(): lax.all_to_all(jnp.repeat(filled.reshape(E, capacity, erased.shape[1]), p...  16.7 us
    dot_general x1, matrix products, on_device(): gate_act = jnp.dot(flat_rows, w_gate[0], preferred_element_type=jnp.float32)  15.9 us
    dot_general x1, matrix products, on_device(): jnp.dot(hidden, w_down[0], preferred_element_type=jnp.float32)  13.8 us
    psum x1, blocking collectives, on_device(): lax.psum(jnp.concatenate([gained_in, router_out, mean_in, narrow], axis=0...  13.2 us
    dot_general x1, matrix products, on_device(): up_act = jnp.dot(flat_rows, w_up[0], preferred_element_type=jnp.float32)  12.5 us
  transfers between devices with their start and end apart: 2, of which 2 were waited for; matrix products, arithmetic and copies ran while one was open for 0% of the time, Pallas kernels for 0%

profile of v1, /device:TPU:0, one launch (start us, length us, event | category | flops | bytes accessed | tf_op | source)
XLA Modules:
  0.0 159.8 jit_solution(10361582863395513640)
XLA Ops:
  6.5 0.0 copy-start
  6.5 0.0 copy-start.3
  6.5 0.0 copy-start.2
  6.5 0.0 all-gather.2.cloned.1.call-start
  6.5 1.1 fusion.18
  7.6 1.4 fusion.36
  9.1 1.6 fusion.17
  10.6 1.2 convolution_bitcast_fusion
  11.8 0.0 copy-done
  11.8 1.2 fusion.35
  13.1 13.2 %psum.7 = f32[82,128]{1,0:T(8,128)S(1)} all-reduce(f32[82,128]{1,0:T(8,128)S(1)} %pad_maximum_fusion), channel_id=1, replica_groups=mesh['dp'=8,'tensor'=4] {'tensor'}, use_global_device_ids=true, to_apply=%region_1.2 | all-reduce | flops 10496 | bytes 83968 | tf_op jit(solution)/shard_map/psum | solution.py:43
  26.3 0.2 convolution_subtract_fusion.1
  26.5 1.6 %fusion.15 = bf16[64,1024]{1,0:T(8,128)(2,1)S(1)} fusion(f32[1024,128]{1,0:T(8,128)S(1)} %copy-done, bf16[64,1024]{1,0:T(8,128)(2,1)} %param.11, f32[64]{0:T(128)S(1)} %fusion.34, f32[1024]{0:T(1024)} %param.12, f32[82,128]{1,0:T(8,128)S(1)} %psum.7, f32[128]{0:T(128)S(1)} %slice_bitcast_fusion), kind=kOutput, calls=%fused_computation.11 | convolution fusion | flops 101007360 | bytes 824832 | tf_op jit(solution)/shard_map/dot_general | solution.py:53
  28.2 0.0 copy-done.3
  28.2 0.0 copy-done.2
  28.3 0.1 convert_reduce_fusion
  28.4 0.3 convolution_convert_fusion
  28.7 16.7 %all_to_all.10 = bf16[8,24,1024]{2,1,0:T(8,128)(2,1)} all-to-all(bf16[8,24,1024]{2,1,0:T(8,128)(2,1)S(1)} %bitcast.48), channel_id=1, replica_groups=mesh['dp'=8,'tensor'=4] {'dp'}, dimensions={0} | all-to-all | bytes 786432 | tf_op jit(solution)/shard_map/all_to_all | solution.py:75
  45.4 0.0 all-gather.2.cloned.1.call-update
  45.4 0.0 reduce-scatter.2.cloned.1.call-start
  45.5 18.7 %all-gather.2.cloned.1.call-done = bf16[8,24,4096]{2,1,0:T(8,128)(2,1)} async-done(((bf16[8,24,1024]{2,1,0:T(8,128)(2,1)}), bf16[8,24,4096]{2,1,0:T(8,128)(2,1)}) %all-gather.2.cloned.1.call-update) | async-done | bytes 1572880 | tf_op jit(solution)/shard_map/all_gather | solution.py:82
  64.2 0.0 copy-start.4
  64.2 15.9 %fusion.4 = f32[192,3584]{1,0:T(8,128)S(1)} fusion(bf16[192,4096]{1,0:T(8,128)(2,1)} %bitcast.51, bf16[1,4096,3584]{2,1,0:T(8,128)(2,1)} %param.19), kind=kOutput, calls=%fused_computation.4 | convolution fusion | flops 5637144576 | bytes 33685504 | tf_op jit(solution)/shard_map/dot_general | solution.py:85
  80.1 0.0 copy-done.4
  80.1 12.5 %fusion.9 = bf16[192,3584]{1,0:T(8,128)(2,1)S(1)} fusion(bf16[192,4096]{1,0:T(8,128)(2,1)S(1)} %bitcast.52, bf16[1,4096,3584]{2,1,0:T(8,128)(2,1)} %param.20, f32[192,3584]{1,0:T(8,128)S(1)} %fusion.4), kind=kOutput, calls=%fused_computation.7 | convolution fusion | flops 5641273344 | bytes 35061760 | tf_op jit(solution)/shard_map/dot_general | solution.py:86
  92.6 0.0 copy-start.1
  92.6 13.8 %fusion.12 = bf16[8,24,4096]{2,1,0:T(8,128)(2,1)} fusion(bf16[8,24,3584]{2,1,0:T(8,128)(2,1)S(1)} %bitcast.53, bf16[1,3584,4096]{2,1,0:T(8,128)(2,1)} %param.21), kind=kOutput, calls=%fused_computation.8 | convolution fusion | flops 5637931008 | bytes 32309248 | tf_op jit(solution)/shard_map/dot_general | solution.py:88
  106.4 0.0 reduce-scatter.2.cloned.1.call-update
  106.4 28.1 %reduce-scatter.2.cloned.1.call-done = bf16[8,24,1024]{2,1,0:T(8,128)(2,1)} async-done(((bf16[8,24,4096]{2,1,0:T(8,128)(2,1)}), bf16[8,24,1024]{2,1,0:T(8,128)(2,1)}) %reduce-scatter.2.cloned.1.call-update) | async-done | bytes 393232 | tf_op jit(solution)/shard_map/reduce_scatter | solution.py:91
  134.6 17.4 %all_to_all.11 = bf16[8,24,1024]{2,1,0:T(8,128)(2,1)S(1)} all-to-all(bf16[8,24,1024]{2,1,0:T(8,128)(2,1)} %reduce-scatter.2.cloned.1.call-done), channel_id=1, replica_groups=mesh['dp'=8,'tensor'=4] {'dp'}, dimensions={0} | all-to-all | bytes 786432 | tf_op jit(solution)/shard_map/all_to_all | solution.py:92
  152.0 1.0 convolution_convert_fusion.1
  153.0 0.0 copy-done.1
  (9 shorter events, 0.1 us)
Async XLA Ops:
  6.5 5.3 %copy-start = (f32[1024,128]{1,0:T(8,128)S(1)}, f32[1024,128]{1,0:T(8,128)}, u32[]{:S(2)}) copy-start(f32[1024,128]{1,0:T(8,128)} %param.15) | copy-start | bytes 1572868
  6.5 21.6 %copy-start.3 = (s32[64,2]{0,1:T(2,128)S(1)}, s32[64,2]{0,1:T(2,128)}, u32[]{:S(2)}) copy-start(s32[64,2]{0,1:T(2,128)} %param.18) | copy-start | bytes 1540
  6.5 21.7 %copy-start.2 = (s32[64,2]{0,1:T(2,128)S(1)}, s32[64,2]{0,1:T(2,128)}, u32[]{:S(2)}) copy-start(s32[64,2]{0,1:T(2,128)} %param.17) | copy-start | bytes 1540
  6.5 57.6 %all-gather.2.cloned.1.call-start = ((), (), s32[]{:S(2)}) async-start(), calls=%async_computation.3 | async-start | bytes 1966080 | tf_op jit(solution)/shard_map/all_gather | solution.py:82
  45.4 89.1 %reduce-scatter.2.cloned.1.call-start = ((), (), s32[]{:S(2)}) async-start(), calls=%async_computation.4 | async-start | bytes 1966080 | tf_op jit(solution)/shard_map/reduce_scatter | solution.py:91
  64.2 15.9 %copy-start.4 = (bf16[8,24,4096]{2,1,0:T(8,128)(2,1)S(1)}, bf16[8,24,4096]{2,1,0:T(8,128)(2,1)}, u32[]{:S(2)}) copy-start(bf16[8,24,4096]{2,1,0:T(8,128)(2,1)} %all-gather.2.cloned.1.call-done) | copy-start | bytes 4718596
  92.6 60.4 %copy-start.1 = (f32[1024,128]{1,0:T(8,128)S(1)}, f32[1024,128]{1,0:T(8,128)}, u32[]{:S(2)}) copy-start(f32[1024,128]{1,0:T(8,128)} %param.15) | copy-start | bytes 1572868
Sparse Core Ops, SparseCore 0:
  45.6 18.5 all-gather.1
  106.5 27.9 reduce-scatter.1

commit v2 on v0

v2 whole, which is shorter than its diff:
```python
import functools

import jax
import jax.numpy as jnp
from jax import lax
from jax.experimental import pallas as pl
from jax.experimental.pallas import tpu as pltpu
from jax.sharding import PartitionSpec as P

E = 8
HIGHEST = lax.Precision.HIGHEST
MESH = pl.DeviceIdType.MESH


def layer_kernel(
    n,
    tensors,
    tok_rows,
    capacity,
    chunk,
    span,
    packed,
    gained,
    eraser_out,
    placing,
    w_gate,
    w_up,
    w_down,
    ret,
    stats,
    stat_in,
    filled,
    xbuf,
    xall,
    hidden,
    gbuf,
    ubuf,
    dbuf,
    part_out,
    part_in,
    pair_out,
    pair_in,
    ret_out,
    gate_sem,
    up_sem,
    down_sem,
    stat_send,
    stat_recv,
    a2a_send,
    a2a_recv,
    near_send,
    near_recv,
    far_send,
    far_recv,
    fwd_send,
    fwd_recv,
    part_send,
    part_recv,
    pair_send,
    pair_recv,
    ret_send,
    ret_recv,
):
    dp = lax.axis_index("dp")
    me = lax.axis_index("tensor")
    side = lax.rem(me, 2)
    row = me // 2
    rows_y = tensors // 2
    partner = row * 2 + (1 - side)
    part_count = n // E
    width = gained.shape[1]
    pieces = width // span
    ff_local = w_gate.shape[2]
    gate_chunks = ff_local // chunk
    gate_slots = gbuf.shape[0]
    down_slots = dbuf.shape[0]
    down_chunks = tensors * pieces

    def gate_copy(c):
        slot = lax.rem(c, gate_slots)
        cols = pl.ds(pl.multiple_of(c * chunk, chunk), chunk)
        return (
            pltpu.make_async_copy(w_gate.at[0, :, cols], gbuf.at[slot], gate_sem.at[slot]),
            pltpu.make_async_copy(w_up.at[0, :, cols], ubuf.at[slot], up_sem.at[slot]),
        )

    def down_owner(i):
        g = i // pieces
        far = g < 2 * (rows_y - 1)
        there = lax.rem(row + 1 + g // 2, rows_y)
        return jnp.where(far, there, row) * 2 + jnp.where(
            lax.rem(g, 2) == 0, 1 - side, side
        )

    def down_copy(i):
        slot = lax.rem(i, down_slots)
        start = down_owner(i) * width + lax.rem(i, pieces) * span
        cols = pl.ds(pl.multiple_of(start, span), span)
        return pltpu.make_async_copy(w_down.at[0, :, cols], dbuf.at[slot], down_sem.at[slot])

    def remote(src, dst, send, recv, device):
        return pltpu.make_async_remote_copy(
            src_ref=src,
            dst_ref=dst,
            send_sem=send,
            recv_sem=recv,
            device_id=device,
            device_id_type=MESH,
        )

    def in_row(t):
        return (dp, t)

    def in_column(d):
        return (d, me)

    @pl.loop(0, gate_slots)
    def _(c):
        one, two = gate_copy(c)
        one.start()
        two.start()

    @pl.loop(0, down_slots)
    def _(i):
        down_copy(i).start()

    barrier = pltpu.get_barrier_semaphore()
    for j in range(1, tensors):
        pl.semaphore_signal(
            barrier, inc=1, device_id=in_row(lax.rem(me + j, tensors)), device_id_type=MESH
        )
    for d in range(1, n):
        pl.semaphore_signal(
            barrier, inc=1, device_id=in_column(lax.rem(dp + d, n)), device_id_type=MESH
        )
    pl.semaphore_wait(barrier, tensors - 1 + n - 1)

    stat_copies = [
        remote(
            packed,
            stat_in.at[j - 1],
            stat_send.at[j - 1],
            stat_recv.at[j - 1],
            in_row(lax.rem(me + j, tensors)),
        )
        for j in range(1, tensors)
    ]
    for copy in stat_copies:
        copy.start()
    for copy in stat_copies:
        copy.wait()
    total = packed[...]
    for j in range(tensors - 1):
        total = total + stat_in[j]
    stats[...] = total

    mean_row = tok_rows + 2 * E
    inv = lax.rsqrt(
        stats[mean_row + 1 : mean_row + 2, :tok_rows] / (width * tensors) + 1e-05
    )
    down_index = lax.broadcasted_iota(jnp.int32, (tok_rows, tok_rows), 0)
    over_index = lax.broadcasted_iota(jnp.int32, (tok_rows, tok_rows), 1)
    inv_rms = jnp.sum(
        jnp.where(down_index == over_index, jnp.broadcast_to(inv, (tok_rows, tok_rows)), 0.0),
        axis=1,
        keepdims=True,
    )
    projected = inv_rms * stats[:tok_rows, :] - stats[mean_row : mean_row + 1, :]
    cleaned = inv_rms * gained[...] - lax.dot_general(
        projected,
        eraser_out[...],
        (((1,), (1,)), ((), ())),
        precision=HIGHEST,
        preferred_element_type=jnp.float32,
    )
    erased = cleaned.astype(jnp.bfloat16)
    placed = jnp.dot(placing[...], erased, preferred_element_type=jnp.float32)
    for e in range(E):
        filled[e] = placed[e * capacity : (e + 1) * capacity].astype(jnp.bfloat16)

    a2a = []
    for d in range(1, n):
        to = lax.rem(dp + d, n)
        a2a.append(
            remote(
                filled.at[to // part_count],
                xbuf.at[me, d],
                a2a_send.at[d - 1],
                a2a_recv.at[d - 1],
                in_column(to),
            )
        )
    for copy in a2a:
        copy.start()
    xbuf[me, 0] = filled[dp // part_count]

    near, far, forward = [], [], []
    lag = 2
    for d in range(n + lag):
        if d < n:
            if d > 0:
                a2a[d - 1].wait_recv()
            for j in range(1, rows_y):
                copy = remote(
                    xbuf.at[me, d],
                    xbuf.at[me, d],
                    far_send.at[j - 1, d],
                    far_recv.at[j - 1, d],
                    in_row(lax.rem(row + j, rows_y) * 2 + side),
                )
                copy.start()
                far.append(copy)
            copy = remote(
                xbuf.at[me, d],
                xbuf.at[me, d],
                near_send.at[d],
                near_recv.at[d],
                in_row(partner),
            )
            copy.start()
            near.append(copy)
        if d >= lag:
            b = d - lag
            for j in range(1, rows_y):
                source = lax.rem(row - j + rows_y, rows_y) * 2 + side
                far[b * (rows_y - 1) + j - 1].wait_recv()
                copy = remote(
                    xbuf.at[source, b],
                    xbuf.at[source, b],
                    fwd_send.at[j - 1, b],
                    fwd_recv.at[j - 1, b],
                    in_row(partner),
                )
                copy.start()
                forward.append(copy)
    for copy in near:
        copy.wait_recv()
    for copy in forward:
        copy.wait_recv()

    for t in range(tensors):
        block = xbuf[t].astype(jnp.float32).reshape(n * capacity, width)
        xall[:, t * width : (t + 1) * width] = block.astype(jnp.bfloat16)

    @pl.loop(0, gate_chunks)
    def _(c):
        slot = lax.rem(c, gate_slots)
        one, two = gate_copy(c)
        one.wait()
        gate = jnp.dot(xall[...], gbuf[slot], preferred_element_type=jnp.float32)
        two.wait()
        up = jnp.dot(xall[...], ubuf[slot], preferred_element_type=jnp.float32)
        cols = pl.ds(pl.multiple_of(c * chunk, chunk), chunk)
        hidden[:, cols] = (gate / (1.0 + jnp.exp(-gate)) * up).astype(jnp.bfloat16)

        @pl.when(c + gate_slots < gate_chunks)
        def _():
            first, second = gate_copy(c + gate_slots)
            first.start()
            second.start()

    def down(i):
        slot = lax.rem(i, down_slots)
        down_copy(i).wait()
        result = jnp.dot(hidden[...], dbuf[slot], preferred_element_type=jnp.float32)

        @pl.when(i + down_slots < down_chunks)
        def _():
            down_copy(i + down_slots).start()

        return result

    def part_copy(j, s):
        return remote(
            part_out.at[j, s],
            part_in.at[j, s],
            part_send.at[j, s],
            part_recv.at[j, s],
            in_row(partner),
        )

    def pair_copy(j, s):
        return remote(
            pair_out.at[j, s],
            pair_in.at[j, s],
            pair_send.at[j, s],
            pair_recv.at[j, s],
            in_row(lax.rem(row + 1 + j, rows_y) * 2 + side),
        )

    def ret_copy(d, s):
        return remote(
            ret_out.at[s, d],
            ret.at[dp, s],
            ret_send.at[d - 1, s],
            ret_recv.at[d - 1, s],
            in_column(lax.rem(dp - d + n, n)),
        )

    for j in range(rows_y):

        @pl.loop(0, pieces)
        def _(s, j=j):
            part_out[j, s] = down(2 * j * pieces + s).astype(jnp.bfloat16)
            part_copy(j, s).start()

        if j < rows_y - 1:

            @pl.loop(0, pieces)
            def _(s, j=j):
                mine = down((2 * j + 1) * pieces + s)
                part_copy(j, s).wait_recv()
                pair_out[j, s] = (mine + part_in[j, s].astype(jnp.float32)).astype(jnp.bfloat16)
                pair_copy(j, s).start()

    last = rows_y - 1

    @pl.loop(0, pieces)
    def _(s):
        mine = down((2 * last + 1) * pieces + s)
        part_copy(last, s).wait_recv()
        mine = mine + part_in[last, s].astype(jnp.float32)
        for j in range(last):
            pair_copy(j, s).wait_recv()
            mine = mine + pair_in[j, s].astype(jnp.float32)
        for d in range(n):
            ret_out[s, d] = mine[d * capacity : (d + 1) * capacity].astype(jnp.bfloat16)
        for d in range(1, n):
            ret_copy(d, s).start()
        ret[dp, s] = ret_out[s, 0]

    for copy in a2a:
        copy.wait_send()
    for copy in near + far + forward:
        copy.wait_send()

    @pl.loop(0, pieces)
    def _(s):
        for j in range(rows_y):
            part_copy(j, s).wait_send()
        for j in range(last):
            pair_copy(j, s).wait_send()
        for d in range(1, n):
            ret_copy(d, s).wait_send()
            ret_copy(d, s).wait_recv()


def on_device(
    tokens,
    norm_gain,
    eraser_mean,
    eraser_in,
    eraser_out,
    router,
    expert_ids,
    slots,
    w_gate,
    w_up,
    w_down,
):
    n = lax.axis_size("dp")
    tensors = lax.axis_size("tensor")
    part_count = n // E
    tok_rows, width = tokens.shape
    capacity = 3 * tok_rows // 8
    rank = eraser_in.shape[1]
    values = tokens.astype(jnp.float32)
    gained = values * norm_gain[None, :]
    squares = jnp.sum(values * values, axis=1)
    gained_in = jnp.dot(gained, eraser_in, precision=HIGHEST, preferred_element_type=jnp.float32)
    mean_in = jnp.dot(
        eraser_mean[None, :], eraser_in, precision=HIGHEST, preferred_element_type=jnp.float32
    )
    router_out = jnp.dot(
        router.T, eraser_out, precision=HIGHEST, preferred_element_type=jnp.float32
    )
    routed = jnp.dot(router.T, gained.T, precision=HIGHEST, preferred_element_type=jnp.float32)
    side_pad = ((0, 0), (0, rank - tok_rows))
    packed = jnp.concatenate(
        [
            gained_in,
            router_out,
            jnp.pad(routed, side_pad),
            mean_in,
            jnp.pad(squares[None, :], side_pad),
            jnp.zeros((6, rank), jnp.float32),
        ],
        axis=0,
    )
    kept_mask = slots < capacity
    target = expert_ids * capacity + slots
    columns = jnp.arange(E * capacity, dtype=jnp.int32)
    match = ((target[:, :, None] == columns[None, None, :]) & kept_mask[:, :, None]).astype(
        jnp.float32
    )
    placing = jnp.sum(match, axis=1).T.astype(jnp.bfloat16)

    hidden_local = w_gate.shape[2]
    chunk = 256 if hidden_local % 256 == 0 else 128
    span = 256
    pieces = width // span
    rows_y = tensors // 2
    rows = n * capacity
    full = width * tensors
    gate_slots = min(6, hidden_local // chunk)
    down_slots = min(8, tensors * pieces)
    bf16 = jnp.bfloat16
    dma = pltpu.SemaphoreType.DMA
    vmem = pl.BlockSpec(memory_space=pltpu.VMEM)
    hbm = pl.BlockSpec(memory_space=pl.ANY)
    ret, stats = pl.pallas_call(
        functools.partial(layer_kernel, n, tensors, tok_rows, capacity, chunk, span),
        out_shape=(
            jax.ShapeDtypeStruct((n, pieces, capacity, span), bf16),
            jax.ShapeDtypeStruct(packed.shape, jnp.float32),
        ),
        in_specs=[vmem] * 4 + [hbm] * 3,
        out_specs=(vmem, vmem),
        scratch_shapes=[
            pltpu.VMEM((tensors - 1,) + packed.shape, jnp.float32),
            pltpu.VMEM((E, capacity, width), bf16),
            pltpu.VMEM((tensors, n, capacity, width), bf16),
            pltpu.VMEM((rows, full), bf16),
            pltpu.VMEM((rows, hidden_local), bf16),
            pltpu.VMEM((gate_slots, full, chunk), bf16),
            pltpu.VMEM((gate_slots, full, chunk), bf16),
            pltpu.VMEM((down_slots, hidden_local, span), bf16),
            pltpu.VMEM((rows_y, pieces, rows, span), bf16),
            pltpu.VMEM((rows_y, pieces, rows, span), bf16),
            pltpu.VMEM((rows_y - 1, pieces, rows, span), bf16),
            pltpu.VMEM((rows_y - 1, pieces, rows, span), bf16),
            pltpu.VMEM((pieces, n, capacity, span), bf16),
            dma((gate_slots,)),
            dma((gate_slots,)),
            dma((down_slots,)),
            dma((tensors - 1,)),
            dma((tensors - 1,)),
            dma((n - 1,)),
            dma((n - 1,)),
            dma((n,)),
            dma((n,)),
            dma((rows_y - 1, n)),
            dma((rows_y - 1, n)),
            dma((rows_y - 1, n)),
            dma((rows_y - 1, n)),
            dma((rows_y, pieces)),
            dma((rows_y, pieces)),
            dma((rows_y - 1, pieces)),
            dma((rows_y - 1, pieces)),
            dma((n - 1, pieces)),
            dma((n - 1, pieces)),
        ],
        compiler_params=pltpu.CompilerParams(
            collective_id=0, has_side_effects=True, vmem_limit_bytes=67043328
        ),
        name="layer",
    )(packed, gained, eraser_out, placing, w_gate, w_up, w_down)

    gained_in = stats[:tok_rows]
    router_out = stats[tok_rows : tok_rows + E]
    routed = stats[tok_rows + E : tok_rows + 2 * E, :tok_rows].T
    mean_in = stats[tok_rows + 2 * E]
    squares = stats[tok_rows + 2 * E + 1, :tok_rows]
    inv_rms = lax.rsqrt(squares / full + 1e-05)
    projected = inv_rms[:, None] * gained_in - mean_in[None, :]
    logits = inv_rms[:, None] * routed - jnp.dot(
        projected, router_out.T, precision=HIGHEST, preferred_element_type=jnp.float32
    )
    chosen = (expert_ids[:, :, None] == jnp.arange(E, dtype=jnp.int32)[None, None, :]).astype(
        jnp.float32
    )
    picked = jnp.sum(chosen * logits[:, None, :], axis=2)
    first_gate = jax.nn.sigmoid(picked[:, 0] - picked[:, 1])
    gate_pair = jnp.stack([first_gate, 1.0 - first_gate], axis=1)
    weights = jnp.sum(match * gate_pair[:, :, None], axis=1)
    summed = jnp.sum(
        ret.astype(jnp.float32).reshape(E, part_count, pieces, capacity, span), axis=1
    )
    summed = summed.transpose(0, 2, 1, 3).reshape(E * capacity, width)
    mixed = jnp.dot(weights, summed, precision=HIGHEST, preferred_element_type=jnp.float32)
    return mixed.astype(jnp.bfloat16)


def solution(mesh):
    in_specs = (
        P("dp", "tensor"),
        P("tensor"),
        P("tensor"),
        P("tensor", None),
        P("tensor", None),
        P("tensor", None),
        P("dp", None),
        P("dp", None),
        P("dp", None, "tensor"),
        P("dp", None, "tensor"),
        P("dp", "tensor", None),
    )
    out_specs = P("dp", "tensor")
    return jax.shard_map(
        on_device, mesh=mesh, in_specs=in_specs, out_specs=out_specs, check_vma=False
    )
```

time: 194 us -> 95 us (0.49)
  blocking collectives: 94.2 us -> 0 us
  Pallas kernels: 0 us -> 76.4 us
  matrix products: 46.5 us -> 7.56 us
  waiting for transfers between devices: 36.5 us -> 0 us
  between operations: 13.5 us -> 0.1 us
  local copies, waits for them, and re-layouts: 0.01 us -> 5.06 us
  other arithmetic: 2.64 us -> 5.47 us
    pallas_call x0 -> x1, Pallas kernels: none -> 76.4 us  [on_device(): pl.pallas_call(functools.partial(layer_kernel, n, tensors, tok_rows, capa...]
    all_to_all x2 -> x0, blocking collectives: 68.6 us -> none  [the longest x1 43.1 us: on_device(): lax.all_to_all(jnp.repeat(filled.reshape(E, capacity, full_rows.shape[1])...]
    dot_general x9 -> x6, matrix products: 46.5 us -> 7.56 us  [the longest x1 1.57 us: on_device(): jnp.dot(gained, eraser_in, precision=HIGHEST, preferred_element_type=jnp....]
    reduce_scatter x1 -> x0, waiting for transfers between devices: 36.5 us -> none  [on_device(): lax.psum_scatter(outputs, 'tensor', scatter_dimension=2, tiled=True)]
    psum x2 -> x0, blocking collectives: 19 us -> none  [the longest x1 13.2 us: on_device(): lax.psum((squares, gained_in, mean_in), 'tensor')]
    all_gather x1 -> x0, blocking collectives: 6.7 us -> none  [on_device(): full_rows = lax.all_gather(erased, 'tensor', axis=1, tiled=True)]
    concatenate x0 -> x1, local copies, waits for them, and re-layouts: none -> 2.38 us  [on_device(): jnp.concatenate([gained_in, router_out, jnp.pad(routed, side_pad), mean_i...]
  transfers between devices with their start and end apart: 1 -> 0, of which waited for: 1 -> 0; matrix products, arithmetic and copies ran while one was open for 0% -> 0% of each run, Pallas kernels for 0% -> 0%
where the time goes in v2:
time: 95 us; the launch traced here: 94.6 us
  Pallas kernels  76.4 us (80%)
  matrix products  7.56 us (8%)
  other arithmetic  5.47 us (6%)
  local copies, waits for them, and re-layouts  5.06 us (5%)
    pallas_call x1, Pallas kernels, on_device(): pl.pallas_call(functools.partial(layer_kernel, n, tensors, tok_rows, capa...  76.4 us
    concatenate x1, local copies, waits for them, and re-layouts, on_device(): jnp.concatenate([gained_in, router_out, jnp.pad(routed, side_pad), mean_i...  2.38 us

profile of v2, /device:TPU:0, one launch (start us, length us, event | category | flops | bytes accessed | tf_op | source)
XLA Modules:
  0.0 94.6 jit_solution(14167419317415480144)
XLA Ops:
  0.0 0.7 broadcast_compare_fusion
  0.7 0.0 copy-start.1
  0.7 1.4 %fusion.10 = f32[1,128]{1,0:T(1,128)S(1)} fusion(f32[1024,1]{0,1:T(1,128)} %bitcast.28, f32[1024,128]{1,0:T(8,128)} %param.14), kind=kOutput, calls=%fused_computation.27 | convolution fusion | flops 1572864 | bytes 528896 | tf_op jit(solution)/shard_map/dot_general | solution.py:371
  2.1 0.7 multiply_add_fusion
  2.8 0.0 copy-start
  2.8 1.4 %fusion.9 = f32[8,128]{1,0:T(8,128)S(1)} fusion(f32[1024,8]{0,1:T(8,128)} %param.16, f32[1024,128]{1,0:T(8,128)} %eraser_out.1), kind=kOutput, calls=%fused_computation.26 | convolution fusion | flops 12582912 | bytes 561152 | tf_op jit(solution)/shard_map/dot_general | solution.py:374
  4.2 1.2 %convolution_bitcast_fusion = f32[8,64]{1,0:T(8,128)S(1)} fusion(f32[1024,8]{0,1:T(8,128)} %param.16, bf16[64,1024]{1,0:T(8,128)(2,1)} %param.11, f32[1024]{0:T(1024)} %param.12), kind=kOutput, calls=%fused_computation.2 | convolution fusion | flops 6422528 | bytes 169984 | tf_op jit(solution)/shard_map/dot_general | solution.py:377
  5.4 0.1 copy-done.1
  5.5 0.0 copy-done
  5.5 0.1 convert_reduce_fusion
  5.6 0.7 copy.29
  6.4 1.6 %fusion.2 = f32[64,128]{1,0:T(8,128)S(1)} fusion(f32[1024,128]{1,0:T(8,128)} %param.14, bf16[64,1024]{1,0:T(8,128)(2,1)} %param.11, f32[1024]{0:T(1024)} %param.12), kind=kOutput, calls=%fused_computation.10 | convolution fusion | flops 100794368 | bytes 692224 | tf_op jit(solution)/shard_map/dot_general | solution.py:370
  7.9 1.7 %convert_multiply_fusion.1 = (f32[64,1024]{1,0:T(8,128)}, f32[64]{0:T(128)S(1)}) fusion(bf16[64,1024]{1,0:T(8,128)(2,1)} %param.11, f32[1024]{0:T(1024)} %param.12), kind=kLoop, calls=%fused_computation.4 | loop fusion | flops 262080 | bytes 397568 | tf_op jit(solution)/shard_map/mul | solution.py:368
  9.7 2.4 %concatenate.3.packed = f32[88,128]{1,0:T(8,128)} concatenate(f32[64,128]{1,0:T(8,128)S(1)} %fusion.2, f32[8,128]{1,0:T(8,128)S(1)} %fusion.9, f32[8,128]{1,0:T(8,128)S(1)} %pad.8, f32[1,128]{1,0:T(1,128)S(1)} %fusion.10, f32[1,128]{1,0:T(1,128)S(1)} %pad.9, f32[6,128]{1,0:T(8,128)S(1)} %broadcast_in_dim.5), dimensions={0} | concatenate | bytes 90112 | tf_op jit(solution)/shard_map/concatenate | solution.py:379
  12.1 76.4 %layer.1 = (bf16[8,4,24,256]{3,2,1,0:T(8,128)(2,1)}, f32[88,128]{1,0:T(8,128)}) custom-call(f32[88,128]{1,0:T(8,128)} %concatenate.3.packed, f32[64,1024]{1,0:T(8,128)} %get-tuple-element.11.gained, f32[1024,128]{1,0:T(8,128)} %eraser_out.1, bf16[192,64]{1,0:T(8,128)(2,1)} %bitcast.27, bf16[1,4096,3584]{2,1,0:T(8,128)(2,1)} %w_gate.1, ...), custom_call_target="tpu_custom_call" | custom-call | tf_op jit(solution)/shard_map/layer/pallas_call | solution.py:411
  88.5 1.2 %copy.30 = bf16[8,24,4,256]{3,2,1,0:T(4,128)(2,1)S(1)} copy(bf16[8,24,4,256]{3,1,2,0:T(8,128)(2,1)} %bitcast.26) | data formatting | bytes 786432 | tf_op jit(solution)/shard_map/transpose | solution.py:479
  89.6 0.1 copy.31
  89.7 0.7 slice_bitcast_fusion
  90.4 0.7 rsqrt_bitcast_fusion
  91.0 1.0 %convolution_subtract_fusion = f32[64,8]{0,1:T(8,128)S(1)} fusion(f32[88,128]{1,0:T(8,128)} %get-tuple-element.7, f32[128]{0:T(128)S(1)} %slice_bitcast_fusion, f32[64]{0:T(128)S(1)} %rsqrt_bitcast_fusion), kind=kOutput, calls=%fused_computation.1 | convolution fusion | flops 803840 | bytes 44544 | tf_op jit(solution)/shard_map/dot_general | solution.py:466
  92.0 0.7 select_reduce_fusion.1
  92.8 0.8 select_reduce_fusion
  93.6 1.0 %convolution_convert_fusion = bf16[64,1024]{1,0:T(8,128)(2,1)} fusion(f32[64,192]{1,0:T(8,128)S(1)} %select_reduce_fusion, bf16[192,1024]{1,0:T(8,128)(2,1)S(1)} %bitcast.24), kind=kOutput, calls=%fused_computation | convolution fusion | flops 151060480 | bytes 573440 | tf_op jit(solution)/shard_map/dot_general | solution.py:480
  (5 shorter events, 0.0 us)
Async XLA Ops:
  0.7 4.8 %copy-start.1 = (pred[64,2]{0,1:T(4,128)(4,1)}, pred[64,2]{0,1:T(4,128)(4,1)S(1)}, u32[]{:S(2)}) copy-start(pred[64,2]{0,1:T(4,128)(4,1)S(1)} %broadcast_compare_fusion) | copy-start | bytes 388
  2.8 2.7 %copy-start = (s32[64,2]{0,1:T(2,128)}, s32[64,2]{0,1:T(2,128)S(1)}, u32[]{:S(2)}) copy-start(s32[64,2]{0,1:T(2,128)S(1)} %multiply_add_fusion) | copy-start | bytes 1540

commit v3 on v2

--- a/solution.py
+++ b/solution.py
@@ -19,15 +19,22 @@
     capacity,
     chunk,
     span,
-    packed,
-    gained,
+    tokens,
+    norm_gain,
+    eraser_mean,
+    eraser_in,
     eraser_out,
-    placing,
+    router_t,
+    expert_ids,
+    slots,
     w_gate,
     w_up,
     w_down,
+    out,
+    packed,
+    stats,
+    weights,
     ret,
-    stats,
     stat_in,
     filled,
     xbuf,
@@ -68,7 +75,7 @@
     rows_y = tensors // 2
     partner = row * 2 + (1 - side)
     part_count = n // E
-    width = gained.shape[1]
+    width = tokens.shape[1]
     pieces = width // span
     ff_local = w_gate.shape[2]
     gate_chunks = ff_local // chunk
@@ -133,6 +140,53 @@
         pl.semaphore_signal(
             barrier, inc=1, device_id=in_column(lax.rem(dp + d, n)), device_id_type=MESH
         )
+    down_index = lax.broadcasted_iota(jnp.int32, (tok_rows, tok_rows), 0)
+    over_index = lax.broadcasted_iota(jnp.int32, (tok_rows, tok_rows), 1)
+    diagonal = down_index == over_index
+
+    def to_row(column):
+        wide = jnp.where(diagonal, jnp.broadcast_to(column, (tok_rows, tok_rows)), 0.0)
+        return jnp.sum(wide, axis=0, keepdims=True)
+
+    def to_column(line):
+        wide = jnp.where(diagonal, jnp.broadcast_to(line, (tok_rows, tok_rows)), 0.0)
+        return jnp.sum(wide, axis=1, keepdims=True)
+
+    values = tokens[...].astype(jnp.float32)
+    gained = values * norm_gain[...]
+    mean_row = tok_rows + 2 * E
+    stacked = jnp.concatenate(
+        [gained, jnp.broadcast_to(eraser_mean[...], (8, width))], axis=0
+    )
+    into = jnp.dot(
+        stacked, eraser_in[...], precision=HIGHEST, preferred_element_type=jnp.float32
+    )
+    contract = (((1,), (1,)), ((), ()))
+    packed[...] = jnp.zeros_like(packed)
+    packed[:tok_rows, :] = into[:tok_rows]
+    packed[tok_rows : tok_rows + E, :] = jnp.dot(
+        router_t[...], eraser_out[...], precision=HIGHEST, preferred_element_type=jnp.float32
+    )
+    packed[tok_rows + E : mean_row, :tok_rows] = lax.dot_general(
+        router_t[...], gained, contract, precision=HIGHEST, preferred_element_type=jnp.float32
+    )
+    packed[mean_row : mean_row + 1, :] = into[tok_rows : tok_rows + 1]
+    packed[mean_row + 1 : mean_row + 2, :tok_rows] = to_row(
+        jnp.sum(values * values, axis=1, keepdims=True)
+    )
+
+    choices = []
+    for k in range(2):
+        expert = expert_ids[k : k + 1, :].astype(jnp.float32)
+        slot = slots[k : k + 1, :].astype(jnp.float32)
+        choices.append((expert, slot, slot < capacity))
+    placing_rows = lax.broadcasted_iota(jnp.int32, (E * capacity, tok_rows), 0).astype(jnp.float32)
+    placing = jnp.zeros((E * capacity, tok_rows), jnp.float32)
+    for expert, slot, kept in choices:
+        target = jnp.where(kept, expert * capacity + slot, -1.0)
+        placing = placing + jnp.where(placing_rows == target, 1.0, 0.0)
+    placing = placing.astype(jnp.bfloat16)
+
     pl.semaphore_wait(barrier, tensors - 1 + n - 1)
 
     stat_copies = [
@@ -154,27 +208,20 @@
         total = total + stat_in[j]
     stats[...] = total
 
-    mean_row = tok_rows + 2 * E
     inv = lax.rsqrt(
         stats[mean_row + 1 : mean_row + 2, :tok_rows] / (width * tensors) + 1e-05
     )
-    down_index = lax.broadcasted_iota(jnp.int32, (tok_rows, tok_rows), 0)
-    over_index = lax.broadcasted_iota(jnp.int32, (tok_rows, tok_rows), 1)
-    inv_rms = jnp.sum(
-        jnp.where(down_index == over_index, jnp.broadcast_to(inv, (tok_rows, tok_rows)), 0.0),
-        axis=1,
-        keepdims=True,
-    )
+    inv_rms = to_column(inv)
     projected = inv_rms * stats[:tok_rows, :] - stats[mean_row : mean_row + 1, :]
-    cleaned = inv_rms * gained[...] - lax.dot_general(
+    cleaned = inv_rms * gained - lax.dot_general(
         projected,
         eraser_out[...],
-        (((1,), (1,)), ((), ())),
+        contract,
         precision=HIGHEST,
         preferred_element_type=jnp.float32,
     )
     erased = cleaned.astype(jnp.bfloat16)
-    placed = jnp.dot(placing[...], erased, preferred_element_type=jnp.float32)
+    placed = jnp.dot(placing, erased, preferred_element_type=jnp.float32)
     for e in range(E):
         filled[e] = placed[e * capacity : (e + 1) * capacity].astype(jnp.bfloat16)
 
@@ -193,6 +240,38 @@
     for copy in a2a:
         copy.start()
     xbuf[me, 0] = filled[dp // part_count]
+
+    logits = inv * stats[tok_rows + E : mean_row, :tok_rows] - lax.dot_general(
+        stats[tok_rows : tok_rows + E, :],
+        projected,
+        contract,
+        precision=HIGHEST,
+        preferred_element_type=jnp.float32,
+    )
+    expert_rows = lax.broadcasted_iota(jnp.int32, (E, tok_rows), 0).astype(jnp.float32)
+    picked = [
+        jnp.sum(
+            jnp.where(expert_rows == expert, logits, 0.0),
+            axis=0,
+            keepdims=True,
+        )
+        for expert, slot, kept in choices
+    ]
+    first_gate = to_column(1.0 / (1.0 + jnp.exp(picked[1] - picked[0])))
+    slot_columns = lax.broadcasted_iota(jnp.int32, (tok_rows, n * capacity), 1)
+    slot_columns = slot_columns.astype(jnp.float32)
+    mix = jnp.zeros((tok_rows, n * capacity), jnp.float32)
+    for (expert, slot, kept), gate in zip(choices, (first_gate, 1.0 - first_gate)):
+        for part in range(part_count):
+            target = jnp.where(kept, (expert * part_count + part) * capacity + slot, -1.0)
+            mix = mix + jnp.where(slot_columns == to_column(target), gate, 0.0)
+    high = mix.astype(jnp.bfloat16)
+    rest = mix - high.astype(jnp.float32)
+    middle = rest.astype(jnp.bfloat16)
+    low = (rest - middle.astype(jnp.float32)).astype(jnp.bfloat16)
+    weights[0] = high
+    weights[1] = middle
+    weights[2] = low
 
     near, far, forward = [], [], []
     lag = 2
@@ -329,6 +408,15 @@
             ret_copy(d, s).start()
         ret[dp, s] = ret_out[s, 0]
 
+    for s in range(pieces):
+        for d in range(1, n):
+            ret_copy(d, s).wait_recv()
+        rows = ret[:, s].astype(jnp.float32).reshape(n * capacity, span).astype(jnp.bfloat16)
+        mixed = jnp.dot(weights[2], rows, preferred_element_type=jnp.float32)
+        mixed = mixed + jnp.dot(weights[1], rows, preferred_element_type=jnp.float32)
+        mixed = mixed + jnp.dot(weights[0], rows, preferred_element_type=jnp.float32)
+        out[:, s * span : (s + 1) * span] = mixed.astype(jnp.bfloat16)
+
     for copy in a2a:
         copy.wait_send()
     for copy in near + far + forward:
@@ -342,7 +430,6 @@
             pair_copy(j, s).wait_send()
         for d in range(1, n):
             ret_copy(d, s).wait_send()
-            ret_copy(d, s).wait_recv()
 
 
 def on_device(
@@ -360,41 +447,9 @@
 ):
     n = lax.axis_size("dp")
     tensors = lax.axis_size("tensor")
-    part_count = n // E
     tok_rows, width = tokens.shape
     capacity = 3 * tok_rows // 8
-    rank = eraser_in.shape[1]
-    values = tokens.astype(jnp.float32)
-    gained = values * norm_gain[None, :]
-    squares = jnp.sum(values * values, axis=1)
-    gained_in = jnp.dot(gained, eraser_in, precision=HIGHEST, preferred_element_type=jnp.float32)
-    mean_in = jnp.dot(
-        eraser_mean[None, :], eraser_in, precision=HIGHEST, preferred_element_type=jnp.float32
-    )
-    router_out = jnp.dot(
-        router.T, eraser_out, precision=HIGHEST, preferred_element_type=jnp.float32
-    )
-    routed = jnp.dot(router.T, gained.T, precision=HIGHEST, preferred_element_type=jnp.float32)
-    side_pad = ((0, 0), (0, rank - tok_rows))
-    packed = jnp.concatenate(
-        [
-            gained_in,
-            router_out,
-            jnp.pad(routed, side_pad),
-            mean_in,
-            jnp.pad(squares[None, :], side_pad),
-            jnp.zeros((6, rank), jnp.float32),
-        ],
-        axis=0,
-    )
-    kept_mask = slots < capacity
-    target = expert_ids * capacity + slots
-    columns = jnp.arange(E * capacity, dtype=jnp.int32)
-    match = ((target[:, :, None] == columns[None, None, :]) & kept_mask[:, :, None]).astype(
-        jnp.float32
-    )
-    placing = jnp.sum(match, axis=1).T.astype(jnp.bfloat16)
-
+    stat_shape = (tok_rows + 2 * E + 8, eraser_in.shape[1])
     hidden_local = w_gate.shape[2]
     chunk = 256 if hidden_local % 256 == 0 else 128
     span = 256
@@ -402,22 +457,23 @@
     rows_y = tensors // 2
     rows = n * capacity
     full = width * tensors
-    gate_slots = min(6, hidden_local // chunk)
+    gate_slots = min(8, hidden_local // chunk)
     down_slots = min(8, tensors * pieces)
     bf16 = jnp.bfloat16
     dma = pltpu.SemaphoreType.DMA
     vmem = pl.BlockSpec(memory_space=pltpu.VMEM)
     hbm = pl.BlockSpec(memory_space=pl.ANY)
-    ret, stats = pl.pallas_call(
+    return pl.pallas_call(
         functools.partial(layer_kernel, n, tensors, tok_rows, capacity, chunk, span),
-        out_shape=(
-            jax.ShapeDtypeStruct((n, pieces, capacity, span), bf16),
-            jax.ShapeDtypeStruct(packed.shape, jnp.float32),
-        ),
-        in_specs=[vmem] * 4 + [hbm] * 3,
-        out_specs=(vmem, vmem),
+        out_shape=jax.ShapeDtypeStruct((tok_rows, width), bf16),
+        in_specs=[vmem] * 8 + [hbm] * 3,
+        out_specs=vmem,
         scratch_shapes=[
-            pltpu.VMEM((tensors - 1,) + packed.shape, jnp.float32),
+            pltpu.VMEM(stat_shape, jnp.float32),
+            pltpu.VMEM(stat_shape, jnp.float32),
+            pltpu.VMEM((3, tok_rows, rows), bf16),
+            pltpu.VMEM((n, pieces, capacity, span), bf16),
+            pltpu.VMEM((tensors - 1,) + stat_shape, jnp.float32),
             pltpu.VMEM((E, capacity, width), bf16),
             pltpu.VMEM((tensors, n, capacity, width), bf16),
             pltpu.VMEM((rows, full), bf16),
@@ -454,31 +510,19 @@
             collective_id=0, has_side_effects=True, vmem_limit_bytes=67043328
         ),
         name="layer",
-    )(packed, gained, eraser_out, placing, w_gate, w_up, w_down)
-
-    gained_in = stats[:tok_rows]
-    router_out = stats[tok_rows : tok_rows + E]
-    routed = stats[tok_rows + E : tok_rows + 2 * E, :tok_rows].T
-    mean_in = stats[tok_rows + 2 * E]
-    squares = stats[tok_rows + 2 * E + 1, :tok_rows]
-    inv_rms = lax.rsqrt(squares / full + 1e-05)
-    projected = inv_rms[:, None] * gained_in - mean_in[None, :]
-    logits = inv_rms[:, None] * routed - jnp.dot(
-        projected, router_out.T, precision=HIGHEST, preferred_element_type=jnp.float32
-    )
-    chosen = (expert_ids[:, :, None] == jnp.arange(E, dtype=jnp.int32)[None, None, :]).astype(
-        jnp.float32
-    )
-    picked = jnp.sum(chosen * logits[:, None, :], axis=2)
-    first_gate = jax.nn.sigmoid(picked[:, 0] - picked[:, 1])
-    gate_pair = jnp.stack([first_gate, 1.0 - first_gate], axis=1)
-    weights = jnp.sum(match * gate_pair[:, :, None], axis=1)
-    summed = jnp.sum(
-        ret.astype(jnp.float32).reshape(E, part_count, pieces, capacity, span), axis=1
-    )
-    summed = summed.transpose(0, 2, 1, 3).reshape(E * capacity, width)
-    mixed = jnp.dot(weights, summed, precision=HIGHEST, preferred_element_type=jnp.float32)
-    return mixed.astype(jnp.bfloat16)
+    )(
+        tokens,
+        norm_gain[None, :],
+        eraser_mean[None, :],
+        eraser_in,
+        eraser_out,
+        router.T,
+        expert_ids.T,
+        slots.T,
+        w_gate,
+        w_up,
+        w_down,
+    )
 
 
 def solution(mesh):

time: 95 us -> 78.7 us (0.83)
  matrix products: 7.56 us -> 0 us
  other arithmetic: 5.47 us -> 0 us
  local copies, waits for them, and re-layouts: 5.06 us -> 1.57 us
    dot_general x6 -> x0, matrix products: 7.56 us -> none  [the longest x1 1.57 us: on_device(): jnp.dot(gained, eraser_in, precision=HIGHEST, preferred_element_type=jnp....]
    concatenate x1 -> x0, local copies, waits for them, and re-layouts: 2.38 us -> none  [on_device(): jnp.concatenate([gained_in, router_out, jnp.pad(routed, side_pad), mean_i...]
    mul x1 -> x0, other arithmetic: 1.74 us -> none  [on_device(): gained = values * norm_gain[None, :]]
    reduce_sum x3 -> x0, other arithmetic: 1.62 us -> none  [the longest x1 0.79 us: on_device(): weights = jnp.sum(match * gate_pair[:, :, None], axis=1)]
    unnamed x5 -> x1, local copies, waits for them, and re-layouts: 0.11 us -> 1.57 us
    transpose x1 -> x0, local copies, waits for them, and re-layouts: 1.16 us -> none  [on_device(): summed = summed.transpose(0, 2, 1, 3).reshape(E * capacity, width)]
where the time goes in v3:
time: 78.7 us; the launch traced here: 78.6 us
  Pallas kernels  77 us (98%)
  local copies, waits for them, and re-layouts  1.57 us (2%)
    pallas_call x1, Pallas kernels, on_device(): pl.pallas_call(functools.partial(layer_kernel, n, tensors, tok_rows, capa...  77 us

profile of v3, /device:TPU:0, one launch (start us, length us, event | category | flops | bytes accessed | tf_op | source)
XLA Modules:
  0.0 78.6 jit_solution(4464788508210960634)
XLA Ops:
  0.0 77.0 %layer.1 = bf16[64,1024]{1,0:T(8,128)(2,1)} custom-call(bf16[64,1024]{1,0:T(8,128)(2,1)} %tokens.1, f32[1,1024]{1,0:T(1,128)} %bitcast.6, f32[1,1024]{1,0:T(1,128)} %bitcast.7, f32[1024,128]{1,0:T(8,128)} %eraser_in.1, f32[1024,128]{1,0:T(8,128)} %eraser_out.1, f32[8,1024]{1,0:T(8,128)} %bitcast.5, s32[2,64]{1,0:T(2,128)} %bitcast.8, s32[2,64]{1,0:T(2,128)} %bitcast.9, ...), custom_call_target="tpu_custom_call" | custom-call | tf_op jit(solution)/shard_map/layer/pallas_call | solution.py:466
  77.0 1.6 %copy.13 = bf16[64,1024]{1,0:T(8,128)(2,1)} copy(bf16[64,1024]{1,0:T(8,128)(2,1)} %layer.1) | data formatting | bytes 262144

commit v4 on v3

--- a/solution.py
+++ b/solution.py
@@ -41,7 +41,6 @@
     xall,
     hidden,
     gbuf,
-    ubuf,
     dbuf,
     part_out,
     part_in,
@@ -87,8 +86,8 @@
         slot = lax.rem(c, gate_slots)
         cols = pl.ds(pl.multiple_of(c * chunk, chunk), chunk)
         return (
-            pltpu.make_async_copy(w_gate.at[0, :, cols], gbuf.at[slot], gate_sem.at[slot]),
-            pltpu.make_async_copy(w_up.at[0, :, cols], ubuf.at[slot], up_sem.at[slot]),
+            pltpu.make_async_copy(w_gate.at[0, :, cols], gbuf.at[slot, :, :chunk], gate_sem.at[slot]),
+            pltpu.make_async_copy(w_up.at[0, :, cols], gbuf.at[slot, :, chunk:], up_sem.at[slot]),
         )
 
     def down_owner(i):
@@ -326,9 +325,9 @@
         slot = lax.rem(c, gate_slots)
         one, two = gate_copy(c)
         one.wait()
-        gate = jnp.dot(xall[...], gbuf[slot], preferred_element_type=jnp.float32)
         two.wait()
-        up = jnp.dot(xall[...], ubuf[slot], preferred_element_type=jnp.float32)
+        both = jnp.dot(xall[...], gbuf[slot], preferred_element_type=jnp.float32)
+        gate, up = both[:, :chunk], both[:, chunk:]
         cols = pl.ds(pl.multiple_of(c * chunk, chunk), chunk)
         hidden[:, cols] = (gate / (1.0 + jnp.exp(-gate)) * up).astype(jnp.bfloat16)
 
@@ -452,13 +451,13 @@
     stat_shape = (tok_rows + 2 * E + 8, eraser_in.shape[1])
     hidden_local = w_gate.shape[2]
     chunk = 256 if hidden_local % 256 == 0 else 128
-    span = 256
+    span = min(512, width)
     pieces = width // span
     rows_y = tensors // 2
     rows = n * capacity
     full = width * tensors
-    gate_slots = min(8, hidden_local // chunk)
-    down_slots = min(8, tensors * pieces)
+    gate_slots = min(7, hidden_local // chunk)
+    down_slots = min(4, tensors * pieces)
     bf16 = jnp.bfloat16
     dma = pltpu.SemaphoreType.DMA
     vmem = pl.BlockSpec(memory_space=pltpu.VMEM)
@@ -478,8 +477,7 @@
             pltpu.VMEM((tensors, n, capacity, width), bf16),
             pltpu.VMEM((rows, full), bf16),
             pltpu.VMEM((rows, hidden_local), bf16),
-            pltpu.VMEM((gate_slots, full, chunk), bf16),
-            pltpu.VMEM((gate_slots, full, chunk), bf16),
+            pltpu.VMEM((gate_slots, full, 2 * chunk), bf16),
             pltpu.VMEM((down_slots, hidden_local, span), bf16),
             pltpu.VMEM((rows_y, pieces, rows, span), bf16),
             pltpu.VMEM((rows_y, pieces, rows, span), bf16),

time: 78.7 us -> 67.7 us (0.86)
  Pallas kernels: 77 us -> 66 us
    pallas_call x1, Pallas kernels: 77 us -> 66 us  [on_device(): pl.pallas_call(functools.partial(layer_kernel, n, tensors, tok_rows, capa...]
where the time goes in v4:
time: 67.7 us; the launch traced here: 67.6 us
  Pallas kernels  66 us (97%)
  local copies, waits for them, and re-layouts  1.57 us (2%)
    pallas_call x1, Pallas kernels, on_device(): pl.pallas_call(functools.partial(layer_kernel, n, tensors, tok_rows, capa...  66 us
    unnamed x1, local copies, waits for them, and re-layouts  1.57 us

profile of v4, /device:TPU:0, one launch (start us, length us, event | category | flops | bytes accessed | tf_op | source)
XLA Modules:
  0.0 67.6 jit_solution(247718775307749545)
XLA Ops:
  0.0 66.0 %layer.1 = bf16[64,1024]{1,0:T(8,128)(2,1)} custom-call(bf16[64,1024]{1,0:T(8,128)(2,1)} %tokens.1, f32[1,1024]{1,0:T(1,128)} %bitcast.6, f32[1,1024]{1,0:T(1,128)} %bitcast.7, f32[1024,128]{1,0:T(8,128)} %eraser_in.1, f32[1024,128]{1,0:T(8,128)} %eraser_out.1, f32[8,1024]{1,0:T(8,128)} %bitcast.5, s32[2,64]{1,0:T(2,128)} %bitcast.8, s32[2,64]{1,0:T(2,128)} %bitcast.9, ...), custom_call_target="tpu_custom_call" | custom-call | tf_op jit(solution)/shard_map/layer/pallas_call | solution.py:465
  66.0 1.6 %copy.13 = bf16[64,1024]{1,0:T(8,128)(2,1)} copy(bf16[64,1024]{1,0:T(8,128)(2,1)} %layer.1) | data formatting | bytes 262144
